TPU v7x, 32 devices: a whole 2x2x4 slice. The times are simulated.
32 devices in a mesh: layer: 4 (over x, core), grid: 8 (over z, y).
Axes of the slice: x: 2, y: 2, z: 4, core: 2. Of those that a mesh axis runs over, the one named last changes fastest.
Arguments:
- band_blocks: bfloat16 [80, 9, 128, 128], P('grid'), may hold values from -7 to 7, as said below
- retained: int32 [80, 9], P('grid'), may hold values from 0 to 1, as said below
Outputs:
- purified: bfloat16 [80, 9, 128, 128], P('grid', None, 'layer')
Inputs may be any that keep to these rules, and one draw needn't show every extreme that they name: `band_blocks`: the matrix is symmetric: block slot w of block row i equals the transpose of block slot 8 - w of block row (i + w - 4) mod 80. retained[i, w] = 1 exactly when retained[(i + w - 4) mod 80, 8 - w] = 1; the middle slot w = 4 is 1 in every block row.
All inputs are finite; a program needn't handle non-finite values.
Results may differ from a plain program's by a relative error of at most 0.005.
Values may be sent and summed in bfloat16 or wider, within the bound.
A program may use at most 64 MiB of HBM per device.

v0:
```python
import functools

import jax
import jax.numpy as jnp
from jax import lax
from jax.experimental import pallas as pl
from jax.experimental.pallas import tpu as pltpu
from jax.sharding import PartitionSpec as P

MESH = pl.DeviceIdType.MESH


def purify(dims, x_hbm, r_hbm, o_ref, x_ref, halo, flags, r3, wide, cur, strip, part, part_square,
           send, recv, r_send, r_recv, local):
    layers, grids, rows, reach, block = dims
    piece = block // layers
    band = 2 * reach + 1
    depth = 2 * reach
    tile = 2 * block
    span = reach // 2
    scale = 1.0 / (4.0 * band * block)
    total = rows + 2 * depth
    tiles = rows // 2
    mids = tiles + 2 * span
    centre = mids // 2

    q = lax.axis_index("layer")
    g = lax.axis_index("grid")
    right = lax.rem(g + 1, grids)
    left = lax.rem(g + grids - 1, grids)
    far = lax.rem(q + layers // 2, layers)
    near = q + 1 - 2 * lax.rem(q, 2)

    own_flags = pltpu.make_async_copy(r_hbm, r3.at[1], local.at[0])
    own_flags.start()
    own_blocks = pltpu.make_async_copy(x_hbm, x_ref, local.at[1])
    own_blocks.start()

    barrier = pltpu.get_barrier_semaphore()
    peers = ((q, left), (q, right), (far, g), (near, g))
    for peer in peers:
        pl.semaphore_signal(barrier, inc=1, device_id=peer, device_id_type=MESH)
    pl.semaphore_wait(barrier, len(peers))

    mine = pl.ds(pl.multiple_of(q * piece, piece), piece)
    fars = pl.ds(pl.multiple_of(far * piece, piece), piece)

    def copy(stage, side, j, source, target, peer):
        return pltpu.make_async_remote_copy(
            src_ref=source,
            dst_ref=target,
            send_sem=send.at[stage, side, j],
            recv_sem=recv.at[stage, side, j],
            device_id=peer,
            device_id_type=MESH,
        )

    sides = ((q, right), (q, left))
    copies = {}
    flag_copies = []
    for side in range(2):
        flag_copies.append(
            pltpu.make_async_remote_copy(
                src_ref=r_hbm,
                dst_ref=flags.at[side],
                send_sem=r_send.at[side],
                recv_sem=r_recv.at[side],
                device_id=sides[side],
                device_id_type=MESH,
            )
        )
    for j in range(depth):
        count = min(reach + 1, j + 1)
        for side in range(2):
            there = halo.at[side, j, 0:count, mine, :]
            beyond = halo.at[side, j, 0:count, fars, :]
            if side == 0:
                source = x_hbm.at[rows - 1 - j, reach : reach + count]
            else:
                source = x_hbm.at[j, reach + 1 - count : reach + 1]
            copies[0, side, j] = copy(0, side, j, source.at[:, mine, :], there, sides[side])
            copies[1, side, j] = copy(1, side, j, there, there, (far, g))
            copies[2, side, j] = copy(2, side, j, there, there, (near, g))
            copies[3, side, j] = copy(3, side, j, beyond, beyond, (near, g))
            copies[0, side, j].start()
        if j == 1:
            for side in range(2):
                flag_copies[side].start()

    def forward(*js):
        for j in js:
            for side in range(2):
                copies[0, side, j].wait_recv()
                copies[1, side, j].start()
                copies[2, side, j].start()

    def share(*js):
        for j in js:
            for side in range(2):
                copies[1, side, j].wait_recv()
                copies[3, side, j].start()

    def masked(value, r, w):
        place = r + rows
        return jnp.where(r3[place // rows, place % rows, w] != 0, value, jnp.zeros_like(value))

    def put(r, c, value):
        wide[
            (r + depth) * block : (r + depth + 1) * block,
            (c + depth) * block : (c + depth + 1) * block,
        ] = value

    def build(*js):
        for j in js:
            for side in range(2):
                copies[2, side, j].wait_recv()
                copies[3, side, j].wait_recv()
                count = min(reach + 1, j + 1)
                r = -1 - j if side == 0 else rows + j
                for s in range(count):
                    w = reach + s if side == 0 else reach + 1 - count + s
                    c = r + w - reach
                    value = masked(halo[side, j, s], r, w)
                    put(r, c, value)
                    if c != r:
                        put(c, r, value.T)

    def ranges(d):
        low = max(0, d - span)
        high = min(2 * span, d + span)
        return low, high + 1

    every = range(2 * span + 1)

    def squares(i, which):
        rows_at = slice((i + span) * tile, (i + span + 1) * tile)
        for d in which:
            low, high = ranges(d)
            inner = slice((i + low) * tile, (i + high) * tile)
            columns = slice((i + d) * tile, (i + d + 1) * tile)
            product = jnp.dot(
                wide[rows_at, inner], wide[inner, columns], preferred_element_type=jnp.float32
            )
            for a in range(2):
                for b in range(2):
                    w = 2 * (d - span) + b - a + reach
                    if 0 <= w < band:
                        value = masked(
                            product[a * block : (a + 1) * block, b * block : (b + 1) * block],
                            2 * i - reach + a,
                            w,
                        ).astype(jnp.bfloat16)
                    else:
                        value = jnp.zeros((block, block), jnp.bfloat16)
                    at = d * tile + b * block
                    strip[i, a * block : (a + 1) * block, at : at + block] = value

    def cubes(i):
        rows_at = slice((i + span) * tile, (i + span + 1) * tile)
        for d in every:
            if not 0 <= i + d - span < mids:
                continue
            low, high = ranges(d)
            inner = slice((i + low) * tile, (i + high) * tile)
            columns = slice((i + d) * tile, (i + d + 1) * tile)
            product = jnp.dot(
                strip[i, :, low * tile : high * tile],
                wide[inner, columns],
                preferred_element_type=jnp.float32,
            )
            value = (3.0 * wide[rows_at, columns].astype(jnp.float32) - product * scale) * 0.5
            for a in range(2):
                for b in range(2):
                    w = 2 * (d - span) + b - a + reach
                    if 0 <= w < band:
                        result = masked(
                            value[a * block : (a + 1) * block, b * block : (b + 1) * block],
                            2 * i - reach + a,
                            w,
                        ).astype(jnp.bfloat16)
                    else:
                        result = jnp.zeros((block, block), jnp.bfloat16)
                    down = i * tile + a * block
                    at = (i + d - span) * tile + b * block
                    cur[down : down + block, at : at + block] = result

    def early(i):
        if span <= i < span + tiles:
            return [d for d in every if span <= i + d - span < span + tiles]
        return [d for d in every if (d > span if i < centre else d < span)]

    def rest(i):
        squares(i, [d for d in every if d not in early(i)])
        cubes(i)

    empty = jnp.zeros((block, block), jnp.bfloat16)
    for t in range(total // 2):
        r = 2 * t - depth
        if r + reach + 1 < rows + depth:
            put(r, r + reach + 1, empty)
        if r - reach >= -depth:
            put(r + 1, r - reach, empty)
    own_flags.wait()
    own_blocks.wait()
    for r in range(rows):
        for w in range(band):
            c = r + w - reach
            value = masked(x_ref[r, w], r, w)
            put(r, c, value)
            if c < 0 or c >= rows:
                put(c, r, value.T)

    def gather():
        for r in range(rows):
            start = pl.multiple_of((r + reach) * block + q * piece, piece)
            for c in range(0, mids * 2):
                if 0 <= c - r < band:
                    part[r * piece : (r + 1) * piece, c * block : (c + 1) * block] = cur[
                        pl.ds(start, piece), c * block : (c + 1) * block
                    ]
                else:
                    blank = jnp.zeros((piece, block), jnp.bfloat16)
                    part[r * piece : (r + 1) * piece, c * block : (c + 1) * block] = blank
                    part_square[r * piece : (r + 1) * piece, c * block : (c + 1) * block] = blank

    def columns_of(c, source):
        low, high = max(0, c - span), min(mids, c + span + 1)
        first, last = max(0, c - 2 * span), min(tiles, c + 1)
        product = jnp.dot(
            source[first * 2 * piece : last * 2 * piece, low * tile : high * tile],
            cur[low * tile : high * tile, c * tile : (c + 1) * tile],
            preferred_element_type=jnp.float32,
        )
        for r in range(2 * first, 2 * last):
            for b in range(2):
                w = 2 * c + b - r
                if 0 <= w < band:
                    at = (r - 2 * first) * piece
                    yield r, w, product[at : at + piece, b * block : (b + 1) * block]

    def part_squares(which):
        for c in which:
            for r, w, value in columns_of(c, part):
                part_square[
                    r * piece : (r + 1) * piece, (r + w) * block : (r + w + 1) * block
                ] = masked(value, r, w).astype(jnp.bfloat16)

    squares(centre, every)
    cubes(centre)
    forward(0, 1)
    squares(centre - 1, early(centre - 1))
    forward(2)
    squares(centre + 1, early(centre + 1))
    squares(centre - 2, early(centre - 2))
    forward(3)
    share(0, 1)
    squares(centre + 2, early(centre + 2))
    for side in range(2):
        flag_copies[side].wait_recv()
        landed = pltpu.make_async_copy(flags.at[side], r3.at[2 * side], local.at[0])
        landed.start()
        landed.wait()
    build(0, 1)
    rest(centre - 1)
    forward(4)
    share(2)
    rest(centre + 1)
    share(3)
    forward(5)
    build(2, 3)
    rest(centre - 2)
    forward(6)
    share(4)
    rest(centre + 2)
    forward(7)
    share(5)
    squares(centre - 3, early(centre - 3))
    squares(centre + 3, early(centre + 3))
    gather()
    build(4, 5)
    rest(centre - 3)
    share(6)
    rest(centre + 3)
    share(7)
    squares(centre - 4, early(centre - 4))
    squares(centre + 4, early(centre + 4))
    inner_columns = range(centre - 1, centre + 2)
    part_squares(inner_columns)
    build(6, 7)
    rest(centre - 4)
    rest(centre + 4)
    part_squares([c for c in range(mids) if c not in inner_columns])

    for c in range(mids):
        for r, w, value in columns_of(c, part_square):
            before = part[r * piece : (r + 1) * piece, (r + w) * block : (r + w + 1) * block]
            after = (3.0 * before.astype(jnp.float32) - value * scale) * 0.5
            o_ref[r, w] = masked(after, r, w).astype(jnp.bfloat16)

    for j in range(depth):
        for side in range(2):
            for stage in range(4):
                copies[stage, side, j].wait_send()
    for side in range(2):
        flag_copies[side].wait_send()


def per_device(layers, grids, band_blocks, retained):
    rows, band, block, _ = band_blocks.shape
    reach = (band - 1) // 2
    depth = 2 * reach
    piece = block // layers
    dtype = band_blocks.dtype
    anywhere = pl.BlockSpec(memory_space=pl.ANY)
    tile = 2 * block
    total = (rows + 2 * depth) * block
    middle = (rows + depth) * block
    return pl.pallas_call(
        functools.partial(purify, (layers, grids, rows, reach, block)),
        out_shape=jax.ShapeDtypeStruct((rows, band, piece, block), dtype),
        in_specs=[anywhere, anywhere],
        out_specs=pl.BlockSpec(memory_space=pltpu.VMEM),
        scratch_shapes=[
            pltpu.VMEM((rows, band, block, block), dtype),
            pltpu.VMEM((2, depth, reach + 1, block, block), dtype),
            pltpu.VMEM((2, rows, band), retained.dtype),
            pltpu.SMEM((3, rows, band), retained.dtype),
            pltpu.VMEM((total, total), dtype),
            pltpu.VMEM((middle, middle), dtype),
            pltpu.VMEM((middle // tile, tile, (reach + 1) * tile), dtype),
            pltpu.VMEM((rows * piece, middle), dtype),
            pltpu.VMEM((rows * piece, middle), dtype),
            pltpu.SemaphoreType.DMA((4, 2, depth)),
            pltpu.SemaphoreType.DMA((4, 2, depth)),
            pltpu.SemaphoreType.DMA((2,)),
            pltpu.SemaphoreType.DMA((2,)),
            pltpu.SemaphoreType.DMA((2,)),
        ],
        compiler_params=pltpu.CompilerParams(
            collective_id=0, has_side_effects=True, vmem_limit_bytes=60 * 1024 * 1024
        ),
        name="purify",
    )(band_blocks, retained)


def solution(mesh):
    return jax.shard_map(
        functools.partial(per_device, mesh.shape["layer"], mesh.shape["grid"]),
        mesh=mesh,
        in_specs=(P("grid", None, None, None), P("grid", None)),
        out_specs=P("grid", None, "layer", None),
        check_vma=False,
    )
```

profile of v0, /device:TPU:0, one launch (start us, length us, event | category | flops | bytes accessed | tf_op | source)
XLA Modules:
  0.0 35.8 jit_solution(11875231810531226627)
XLA Ops:
  0.0 33.7 %purify.1 = bf16[10,9,32,128]{3,2,1,0:T(8,128)(2,1)} custom-call(bf16[10,9,128,128]{3,2,1,0:T(8,128)(2,1)} %x_hbm.1, s32[10,9]{1,0:T(8,128)} %r_hbm.1), custom_call_target="tpu_custom_call" | custom-call | tf_op jit(solution)/shard_map/purify/pallas_call | solution.py:318
  33.7 2.0 %copy.4 = bf16[10,9,32,128]{3,2,1,0:T(8,128)(2,1)} copy(bf16[10,9,32,128]{3,2,1,0:T(8,128)(2,1)} %purify.1) | data formatting | bytes 1474560
where the time goes:
time: 35.9 us; the launch traced here: 35.8 us
  Pallas kernels  33.7 us (94%)
  local copies, waits for them, and re-layouts  2.03 us (6%)
    pallas_call x1, Pallas kernels, per_device(): pl.pallas_call(functools.partial(purify, (layers, grids, rows, reach, blo...  33.7 us
    unnamed x1, local copies, waits for them, and re-layouts  2.03 us

commit v1 on v0

v1 whole, which is shorter than its diff:
```python
import functools

import jax
import jax.numpy as jnp
from jax import lax
from jax.experimental import pallas as pl
from jax.experimental.pallas import tpu as pltpu
from jax.sharding import PartitionSpec as P

MESH = pl.DeviceIdType.MESH


def purify(dims, x_hbm, r_hbm, o_ref, x_ref, halo, flags, r2, wide, cur, strip, part, part_square,
           outbox, y_send, y_recv, x_send, x_recv, c_send, c_recv, o_send, o_recv, r_send, r_recv,
           local, local_flags):
    layers, grids, rows, reach, block = dims
    piece = block // layers
    pair = 2 * piece
    band = 2 * reach + 1
    depth = 2 * reach
    tile = 2 * block
    span = reach // 2
    half = rows // 2
    scale = 1.0 / (4.0 * band * block)
    last = (depth + half - 1) // 2
    tiles = last + span + 1
    own = reach
    edge = own - span

    q = lax.axis_index("layer")
    g = lax.axis_index("grid")
    core = lax.rem(q, 2)
    base = q - core
    right = lax.rem(g + 1, grids)
    left = lax.rem(g + grids - 1, grids)
    far = lax.rem(q + layers // 2, layers)
    near = base + 1 - core
    outer = jnp.where(core == 0, left, right)
    inner = jnp.where(core == 0, right, left)

    def mirror(i, count):
        return i + core * (count - 1 - 2 * i)

    def strip_of(index, size):
        return pl.ds(pl.multiple_of(index * size, size), size)

    own_flags = pltpu.make_async_copy(r_hbm, r2.at[0], local_flags.at[0])
    own_flags.start()
    order = range(rows)
    own_rows = [
        pltpu.make_async_copy(
            x_hbm.at[mirror(r, rows)], x_ref.at[mirror(r, rows)], local.at[r]
        )
        for r in order
    ]
    for r in order:
        own_rows[r].start()

    barrier = pltpu.get_barrier_semaphore()
    peers = ((base, outer), (base + 1, outer), (far, g), (near, g))
    for peer in peers:
        pl.semaphore_signal(barrier, inc=1, device_id=peer, device_id_type=MESH)

    def remote(source, target, send_sem, recv_sem, peer):
        return pltpu.make_async_remote_copy(
            src_ref=source,
            dst_ref=target,
            send_sem=send_sem,
            recv_sem=recv_sem,
            device_id=peer,
            device_id_type=MESH,
        )

    mine = strip_of(q, piece)
    plane = lax.div(q, 2)
    near_rows = strip_of(plane, pair)
    far_rows = strip_of(lax.div(far, 2), pair)
    sides = ((base, right), (base + 1, left))
    sends = {}
    arrivals = {}
    crossings = {}
    landings = {}
    for j in range(depth):
        count = min(reach + 1, j + 1)
        for side in range(2):
            if side == 0:
                source = x_hbm.at[rows - 1 - j, reach : reach + count, mine, :]
            else:
                source = x_hbm.at[j, reach + 1 - count : reach + 1, mine, :]
            there = halo.at[j, 0:count, mine, :]
            sends[side, j] = remote(
                source, there, y_send.at[side, j], y_recv.at[core, j], sides[side]
            )
        for p in range(2):
            here = halo.at[j, 0:count, strip_of(base + p, piece), :]
            arrivals[p, j] = remote(here, here, y_send.at[p, j], y_recv.at[p, j], (near, g))
        across = halo.at[j, 0:count, near_rows, :]
        crossings[j] = remote(across, across, x_send.at[j], x_recv.at[j], (far, g))
        beyond = halo.at[j, 0:count, far_rows, :]
        landings[j] = remote(beyond, beyond, x_send.at[j], x_recv.at[j], (far, g))
    flag_copy = remote(r_hbm, flags, r_send, r_recv, (q, inner))

    def at(r):
        return slice((r + depth) * block, (r + depth + 1) * block)

    def cur_at(r):
        return slice((r + reach) * block, (r + reach + 1) * block)

    def masked(value, r, w):
        kept = r2[0 if r >= 0 else 1, mirror(r % rows, rows), mirror(w, band)]
        return jnp.where(kept != 0, value, jnp.zeros_like(value))

    def put(r, c, value):
        wide[at(r), at(c)] = value

    empty = jnp.zeros((block, block), jnp.bfloat16)
    blank = jnp.zeros((pair, block), jnp.bfloat16)

    def height(i):
        return min(2, depth + half - 2 * i)

    def extent(i, c):
        return max(i, c) - span, min(i, c) + span + 1

    def squares(i, columns):
        m = height(i)
        lines = slice(i * tile, i * tile + m * block)
        for c in columns:
            low, high = extent(i, c)
            product = jnp.dot(
                wide[lines, low * tile : high * tile],
                wide[low * tile : high * tile, c * tile : (c + 1) * tile],
                preferred_element_type=jnp.float32,
            )
            for a in range(m):
                for b in range(2):
                    w = 2 * (c - i) + b - a + reach
                    if 0 <= w < band:
                        value = masked(
                            product[a * block : (a + 1) * block, b * block : (b + 1) * block],
                            2 * i - depth + a,
                            w,
                        ).astype(jnp.bfloat16)
                    else:
                        value = empty
                    to = (c - i + span) * tile + b * block
                    strip[i - edge, a * block : (a + 1) * block, to : to + block] = value

    def cubes(i, columns):
        m = height(i)
        lines = slice(i * tile, i * tile + m * block)
        for k in columns:
            low, high = extent(i, k)
            product = jnp.dot(
                strip[
                    i - edge, 0 : m * block, (low - i + span) * tile : (high - i + span) * tile
                ],
                wide[low * tile : high * tile, k * tile : (k + 1) * tile],
                preferred_element_type=jnp.float32,
            )
            before = wide[lines, k * tile : (k + 1) * tile].astype(jnp.float32)
            after = (3.0 * before - product * scale) * 0.5
            for a in range(m):
                r = 2 * i - depth + a
                for b in range(2):
                    c = 2 * k - depth + b
                    w = c - r + reach
                    if 0 <= w < band:
                        value = masked(
                            after[a * block : (a + 1) * block, b * block : (b + 1) * block], r, w
                        ).astype(jnp.bfloat16)
                    else:
                        value = empty
                    cur[cur_at(r), cur_at(c)] = value

    def part_at(r):
        return slice(r * pair, (r + 1) * pair)

    def gather(i):
        for a in range(height(i)):
            r = 2 * i - depth + a
            for k in range(i - span, i + span + 1):
                for b in range(2):
                    c = 2 * k - depth + b
                    if abs(c - r) <= reach:
                        for p, layer in enumerate((q, near)):
                            start = (r + reach) * block + layer * piece
                            part[r * pair + p * piece : r * pair + (p + 1) * piece, cur_at(c)] = (
                                cur[pl.ds(pl.multiple_of(start, piece), piece), cur_at(c)]
                            )
                    else:
                        part[part_at(r), cur_at(c)] = blank

    def part_product(source, i, k):
        low, high = extent(i, k)
        lines = slice((2 * i - depth) * pair, (2 * i - depth + height(i)) * pair)
        inside = slice((low - edge) * tile, (high - edge) * tile)
        product = jnp.dot(
            source[lines, inside],
            cur[inside, (k - edge) * tile : (k - edge + 1) * tile],
            preferred_element_type=jnp.float32,
        )
        for a in range(height(i)):
            for b in range(2):
                r = 2 * i - depth + a
                c = 2 * k - depth + b
                yield r, c, product[a * pair : (a + 1) * pair, b * block : (b + 1) * block]

    def part_squares(i, columns):
        for k in columns:
            for r, c, value in part_product(part, i, k):
                if abs(c - r) <= reach:
                    value = masked(value, r, c - r + reach).astype(jnp.bfloat16)
                else:
                    value = blank
                part_square[part_at(r), cur_at(c)] = value

    def finish(i):
        for k in range(i - span, i + span + 1):
            for r, c, value in part_product(part_square, i, k):
                w = c - r + reach
                if not 0 <= w < band:
                    continue
                before = part[part_at(r), cur_at(c)].astype(jnp.float32)
                after = masked((3.0 * before - value * scale) * 0.5, r, w).astype(jnp.bfloat16)
                o_ref[mirror(r, rows), mirror(w, band)] = after[:piece]
                outbox[r, mirror(w, band)] = after[piece:]

    results = [
        remote(
            outbox.at[r], o_ref.at[mirror(r, rows)], o_send.at[r], o_recv.at[r], (near, g)
        )
        for r in range(half)
    ]
    returned = [
        remote(
            outbox.at[r],
            o_ref.at[mirror(rows - 1 - r, rows)],
            o_send.at[r],
            o_recv.at[r],
            (near, g),
        )
        for r in range(half)
    ]

    exchanges = {}
    partners = {}
    n = 0
    for r in range(half - 1, half - 1 - reach, -1):
        for c in range(rows - half - reach, r + reach + 1):
            there = cur.at[cur_at(rows - 1 - r), cur_at(rows - 1 - c)]
            exchanges[r, c] = remote(
                cur.at[cur_at(r), cur_at(c)], there, c_send.at[n], c_recv.at[n], (near, g)
            )
            partners[r, c] = remote(there, there, c_send.at[n], c_recv.at[n], (near, g))
            n += 1

    def exchange(*rs):
        for r, c in exchanges:
            if r in rs:
                exchanges[r, c].start()

    def forward(*js):
        for j in js:
            for p in range(2):
                arrivals[p, j].wait_recv()
            crossings[j].start()

    def build(*js):
        for j in js:
            landings[j].wait_recv()
            count = min(reach + 1, j + 1)
            r = -1 - j
            for s in range(count):
                c = r + s
                value = masked(halo[j, mirror(s, count)], r, reach + s)
                put(r, c, value)
                if c != r:
                    put(c, r, value.T)

    for t in range(tiles):
        r = 2 * t - depth
        if t + span < tiles:
            put(r, r + reach + 1, empty)
        if t >= span:
            put(r + 1, r - reach, empty)
    for r in range(half, 2 * tiles - depth):
        t = (r + depth) // 2
        for k in range(t - span, min(t + span + 1, tiles)):
            for b in range(2):
                c = 2 * k - depth + b
                if (rows - 1 - r, rows - 1 - c) not in exchanges:
                    cur[cur_at(r), cur_at(c)] = empty

    own_flags.wait()
    for r in order:
        own_rows[r].wait()
        for w in range(band):
            c = r + w - reach
            if c >= 2 * tiles - depth:
                continue
            value = masked(x_ref[mirror(r, rows), mirror(w, band)], r, w)
            put(r, c, value)
            if c < 0:
                put(c, r, value.T)

    pl.semaphore_wait(barrier, len(peers))
    for j in range(depth):
        for side in range(2):
            sends[side, j].start()
        if j == 1:
            flag_copy.start()

    i = last
    squares(i, range(i - span, i + span + 1))
    cubes(i, range(i - span, i + span + 1))
    squares(i - 1, range(i - span, i + 2))
    exchange(half - 1)
    squares(i - 2, range(i - 2, i + 1))
    cubes(i - 1, range(i, i + 2))
    forward(0, 1)
    cubes(i - 2, range(i, i + 1))
    forward(2)
    gather(i)
    flag_copy.wait_recv()
    landed = pltpu.make_async_copy(flags, r2.at[1], local_flags.at[1])
    landed.start()
    landed.wait()
    build(0, 1)
    forward(3)
    squares(i - 1, [i - 3])
    squares(i - 3, [i - 1])
    cubes(i - 1, range(i - 3, i))
    forward(4)
    build(2, 3)
    exchange(half - 2, half - 3)
    squares(i - 2, [i - 4, i - 3])
    squares(i - 3, [i - 2])
    squares(i - 4, [i - 2])
    forward(5)
    cubes(i - 2, range(i - 4, i))
    gather(i - 1)
    gather(i - 2)
    exchange(half - 4)
    forward(6)
    build(4, 5)
    squares(i - 3, range(i - 5, i - 2))
    squares(i - 4, [i - 3])
    for r, c in partners:
        partners[r, c].wait_recv()
    part_squares(i, range(i - span, i + span + 1))
    cubes(i - 3, range(i - 4, i))
    forward(7)
    finish(i)
    part_squares(i - 1, range(i - 3, i + 2))
    results[half - 1].start()
    finish(i - 1)
    part_squares(i - 2, range(i - 1, i + 1))
    results[half - 2].start()
    results[half - 3].start()
    build(6, 7)
    squares(i - 4, range(i - 6, i - 3))
    cubes(i - 4, range(i - 4, i - 1))
    part_squares(i - 2, range(i - 4, i - 1))
    finish(i - 2)
    results[half - 4].start()
    results[half - 5].start()

    for r in range(half):
        returned[r].wait_recv()
    for j in range(depth):
        for side in range(2):
            sends[side, j].wait_send()
        crossings[j].wait_send()
    for key in exchanges:
        exchanges[key].wait_send()
    for r in range(half):
        results[r].wait_send()
    flag_copy.wait_send()


def per_device(layers, grids, band_blocks, retained):
    rows, band, block, _ = band_blocks.shape
    reach = (band - 1) // 2
    depth = 2 * reach
    half = rows // 2
    piece = block // layers
    pair = 2 * piece
    dtype = band_blocks.dtype
    outside = pl.BlockSpec(memory_space=pltpu.HBM)
    tile = 2 * block
    span = reach // 2
    last = (depth + half - 1) // 2
    tiles = last + span + 1
    window = (tiles - reach + span) * tile
    swaps = sum(r + 2 * reach + 1 - rows + half for r in range(half - reach, half))
    dma = pltpu.SemaphoreType.DMA
    return pl.pallas_call(
        functools.partial(purify, (layers, grids, rows, reach, block)),
        out_shape=jax.ShapeDtypeStruct((rows, band, piece, block), dtype),
        in_specs=[outside, outside],
        out_specs=pl.BlockSpec(memory_space=pltpu.VMEM),
        scratch_shapes=[
            pltpu.VMEM((rows, band, block, block), dtype),
            pltpu.VMEM((depth, reach + 1, block, block), dtype),
            pltpu.VMEM((rows, band), retained.dtype),
            pltpu.SMEM((2, rows, band), retained.dtype),
            pltpu.VMEM((tiles * tile, tiles * tile), dtype),
            pltpu.VMEM((window, window), dtype),
            pltpu.VMEM((last - reach + span + 1, tile, (reach + 1) * tile), dtype),
            pltpu.VMEM((half * pair, window), dtype),
            pltpu.VMEM((half * pair, window), dtype),
            pltpu.VMEM((half, band, piece, block), dtype),
            dma((2, depth)),
            dma((2, depth)),
            dma((depth,)),
            dma((depth,)),
            dma((swaps,)),
            dma((swaps,)),
            dma((half,)),
            dma((half,)),
            dma,
            dma,
            dma((rows,)),
            dma((2,)),
        ],
        compiler_params=pltpu.CompilerParams(
            collective_id=0, has_side_effects=True, vmem_limit_bytes=44 * 1024 * 1024
        ),
        name="purify",
    )(band_blocks, retained)


def solution(mesh):
    return jax.shard_map(
        functools.partial(per_device, mesh.shape["layer"], mesh.shape["grid"]),
        mesh=mesh,
        in_specs=(P("grid", None, None, None), P("grid", None)),
        out_specs=P("grid", None, "layer", None),
        check_vma=False,
    )
```

time: 35.9 us -> 35 us (0.975); the launches traced: 35.8 us -> 34.3 us
  Pallas kernels: 33.7 us -> 30.9 us
  local copies, waits for them, and re-layouts: 2.03 us -> 3.39 us
    pallas_call x1, Pallas kernels: 33.7 us -> 30.9 us  [per_device(): pl.pallas_call(functools.partial(purify, (layers, grids, rows, reach, blo...]
    unnamed x1 -> x5, local copies, waits for them, and re-layouts: 2.03 us -> 3.39 us
where the time goes in v1:
time: 35 us; the launch traced here: 34.3 us
  Pallas kernels  30.9 us (88%)
  local copies, waits for them, and re-layouts  3.39 us (10%)
    pallas_call x1, Pallas kernels, per_device(): pl.pallas_call(functools.partial(purify, (layers, grids, rows, reach, blo...  30.9 us
    unnamed x5, local copies, waits for them, and re-layouts  3.39 us

profile of v1, /device:TPU:0, one launch (start us, length us, event | category | flops | bytes accessed | tf_op | source)
XLA Modules:
  0.0 34.3 jit_solution(1299413830616401450)
XLA Ops:
  0.0 0.0 copy-start
  0.0 1.8 %copy-done = bf16[10,9,128,128]{3,2,1,0:T(8,128)(2,1)S(1)} copy-done((bf16[10,9,128,128]{3,2,1,0:T(8,128)(2,1)S(1)}, bf16[10,9,128,128]{3,2,1,0:T(8,128)(2,1)}, u32[]{:S(2)}) %copy-start) | copy-done | bytes 2949144
  1.8 0.0 copy-start.1
  1.8 0.7 %copy-done.1 = s32[10,9]{1,0:T(8,128)S(1)} copy-done((s32[10,9]{1,0:T(8,128)S(1)}, s32[10,9]{1,0:T(8,128)}, u32[]{:S(2)}) %copy-start.1) | copy-done | bytes 384
  2.5 30.9 %purify.1 = bf16[10,9,32,128]{3,2,1,0:T(8,128)(2,1)S(1)} custom-call(bf16[10,9,128,128]{3,2,1,0:T(8,128)(2,1)S(1)} %copy-done, s32[10,9]{1,0:T(8,128)S(1)} %copy-done.1), custom_call_target="tpu_custom_call" | custom-call | tf_op jit(solution)/shard_map/purify/pallas_call | solution.py:398
  33.5 0.9 %copy.4 = bf16[10,9,32,128]{3,2,1,0:T(8,128)(2,1)} copy(bf16[10,9,32,128]{3,2,1,0:T(8,128)(2,1)S(1)} %purify.1) | data formatting | bytes 1474560
Async XLA Ops:
  0.0 1.8 %copy-start = (bf16[10,9,128,128]{3,2,1,0:T(8,128)(2,1)S(1)}, bf16[10,9,128,128]{3,2,1,0:T(8,128)(2,1)}, u32[]{:S(2)}) copy-start(bf16[10,9,128,128]{3,2,1,0:T(8,128)(2,1)} %x_hbm.1) | copy-start | bytes 8847364
  1.8 0.7 %copy-start.1 = (s32[10,9]{1,0:T(8,128)S(1)}, s32[10,9]{1,0:T(8,128)}, u32[]{:S(2)}) copy-start(s32[10,9]{1,0:T(8,128)} %r_hbm.1) | copy-start | bytes 1084

commit v2 on v1

--- a/solution.py
+++ b/solution.py
@@ -12,7 +12,7 @@
 
 def purify(dims, x_hbm, r_hbm, o_ref, x_ref, halo, flags, r2, wide, cur, strip, part, part_square,
            outbox, y_send, y_recv, x_send, x_recv, c_send, c_recv, o_send, o_recv, r_send, r_recv,
-           local, local_flags):
+           local, local_flags, ready):
     layers, grids, rows, reach, block = dims
     piece = block // layers
     pair = 2 * piece
@@ -57,9 +57,25 @@
         own_rows[r].start()
 
     barrier = pltpu.get_barrier_semaphore()
-    peers = ((base, outer), (base + 1, outer), (far, g), (near, g))
-    for peer in peers:
-        pl.semaphore_signal(barrier, inc=1, device_id=peer, device_id_type=MESH)
+    first = g == 0
+    final = g == grids - 1
+    closing = jnp.logical_and(final, core == 1)
+    opening = jnp.logical_and(first, core == 1)
+
+    def signal(semaphore, peer):
+        pl.semaphore_signal(semaphore, inc=1, device_id=peer, device_id_type=MESH)
+
+    @pl.when(jnp.logical_not(closing))
+    def _():
+        signal(barrier, (base, outer))
+        signal(barrier, (base + 1, outer))
+
+    @pl.when(opening)
+    def _():
+        signal(barrier, (base + 1, left))
+
+    signal(barrier, (far, g))
+    signal(barrier, (near, g))
 
     def remote(source, target, send_sem, recv_sem, peer):
         return pltpu.make_async_remote_copy(
@@ -292,6 +308,33 @@
                 if (rows - 1 - r, rows - 1 - c) not in exchanges:
                     cur[cur_at(r), cur_at(c)] = empty
 
+    pl.semaphore_wait(barrier, 4 + closing.astype(jnp.int32) - first.astype(jnp.int32))
+
+    @pl.when(closing)
+    def _():
+        signal(ready, (base, right))
+        signal(ready, (base + 1, right))
+
+    @pl.when(jnp.logical_or(first, final))
+    def _():
+        for j in range(depth):
+            sends[0, j].start()
+
+    @pl.when(final)
+    def _():
+        for j in range(depth):
+            sends[1, j].start()
+
+    @pl.when(jnp.logical_not(jnp.logical_or(first, final)))
+    def _():
+        for j in range(depth):
+            for side in range(2):
+                sends[side, j].start()
+
+    @pl.when(jnp.logical_not(opening))
+    def _():
+        flag_copy.start()
+
     own_flags.wait()
     for r in order:
         own_rows[r].wait()
@@ -304,56 +347,61 @@
             if c < 0:
                 put(c, r, value.T)
 
-    pl.semaphore_wait(barrier, len(peers))
-    for j in range(depth):
-        for side in range(2):
-            sends[side, j].start()
-        if j == 1:
-            flag_copy.start()
 
     i = last
     squares(i, range(i - span, i + span + 1))
     cubes(i, range(i - span, i + span + 1))
+
+    @pl.when(first)
+    def _():
+        pl.semaphore_wait(ready, 1)
+        for j in range(depth):
+            sends[1, j].start()
+
+    @pl.when(opening)
+    def _():
+        flag_copy.start()
+
+    forward(0, 1)
     squares(i - 1, range(i - span, i + 2))
     exchange(half - 1)
+    forward(2)
     squares(i - 2, range(i - 2, i + 1))
     cubes(i - 1, range(i, i + 2))
-    forward(0, 1)
     cubes(i - 2, range(i, i + 1))
-    forward(2)
     gather(i)
+    forward(3)
     flag_copy.wait_recv()
     landed = pltpu.make_async_copy(flags, r2.at[1], local_flags.at[1])
     landed.start()
     landed.wait()
     build(0, 1)
-    forward(3)
     squares(i - 1, [i - 3])
     squares(i - 3, [i - 1])
+    forward(4)
     cubes(i - 1, range(i - 3, i))
-    forward(4)
+    exchange(half - 2, half - 3)
+    forward(5)
     build(2, 3)
-    exchange(half - 2, half - 3)
     squares(i - 2, [i - 4, i - 3])
     squares(i - 3, [i - 2])
     squares(i - 4, [i - 2])
-    forward(5)
     cubes(i - 2, range(i - 4, i))
     gather(i - 1)
     gather(i - 2)
     exchange(half - 4)
     forward(6)
+    for r, c in partners:
+        partners[r, c].wait_recv()
+    part_squares(i, range(i - span, i + span + 1))
+    forward(7)
+    finish(i)
+    results[half - 1].start()
     build(4, 5)
     squares(i - 3, range(i - 5, i - 2))
     squares(i - 4, [i - 3])
-    for r, c in partners:
-        partners[r, c].wait_recv()
-    part_squares(i, range(i - span, i + span + 1))
     cubes(i - 3, range(i - 4, i))
-    forward(7)
-    finish(i)
     part_squares(i - 1, range(i - 3, i + 2))
-    results[half - 1].start()
     finish(i - 1)
     part_squares(i - 2, range(i - 1, i + 1))
     results[half - 2].start()
@@ -423,12 +471,13 @@
             dma,
             dma((rows,)),
             dma((2,)),
+            pltpu.SemaphoreType.REGULAR,
         ],
         compiler_params=pltpu.CompilerParams(
             collective_id=0, has_side_effects=True, vmem_limit_bytes=44 * 1024 * 1024
         ),
         name="purify",
-    )(band_blocks, retained)
+    )(pltpu.with_memory_space_constraint(band_blocks, pltpu.HBM), pltpu.with_memory_space_constraint(retained, pltpu.HBM))
 
 
 def solution(mesh):

time: 35 us -> 29.7 us (0.85); the launches traced: 34.3 us -> 29.5 us
  local copies, waits for them, and re-layouts: 3.39 us -> 0.87 us
  Pallas kernels: 30.9 us -> 28.7 us
    unnamed x5 -> x1, local copies, waits for them, and re-layouts: 3.39 us -> 0.87 us
    pallas_call x1, Pallas kernels: 30.9 us -> 28.7 us  [per_device(): pl.pallas_call(functools.partial(purify, (layers, grids, rows, reach, blo...]
where the time goes in v2:
time: 29.7 us; the launch traced here: 29.5 us
  Pallas kernels  28.7 us (97%)
  local copies, waits for them, and re-layouts  0.87 us (3%)
    pallas_call x1, Pallas kernels, per_device(): pl.pallas_call(functools.partial(purify, (layers, grids, rows, reach, blo...  28.7 us
    unnamed x1, local copies, waits for them, and re-layouts  0.87 us

profile of v2, /device:TPU:0, one launch (start us, length us, event | category | flops | bytes accessed | tf_op | source)
XLA Modules:
  0.0 29.5 jit_solution(9386747503651282161)
XLA Ops:
  0.0 28.7 %purify.1 = bf16[10,9,32,128]{3,2,1,0:T(8,128)(2,1)S(1)} custom-call(bf16[10,9,128,128]{3,2,1,0:T(8,128)(2,1)} %x_hbm.1, s32[10,9]{1,0:T(8,128)} %r_hbm.1), custom_call_target="tpu_custom_call" | custom-call | tf_op jit(solution)/shard_map/purify/pallas_call | solution.py:446
  28.7 0.9 %copy.4 = bf16[10,9,32,128]{3,2,1,0:T(8,128)(2,1)} copy(bf16[10,9,32,128]{3,2,1,0:T(8,128)(2,1)S(1)} %purify.1) | data formatting | bytes 1474560

commit v3 on v2

--- a/solution.py
+++ b/solution.py
@@ -315,6 +315,10 @@
         signal(ready, (base, right))
         signal(ready, (base + 1, right))
 
+    @pl.when(jnp.logical_not(opening))
+    def _():
+        flag_copy.start()
+
     @pl.when(jnp.logical_or(first, final))
     def _():
         for j in range(depth):
@@ -330,10 +334,6 @@
         for j in range(depth):
             for side in range(2):
                 sends[side, j].start()
-
-    @pl.when(jnp.logical_not(opening))
-    def _():
-        flag_copy.start()
 
     own_flags.wait()
     for r in order:
@@ -355,12 +355,13 @@
     @pl.when(first)
     def _():
         pl.semaphore_wait(ready, 1)
+
+        @pl.when(core == 1)
+        def _():
+            flag_copy.start()
+
         for j in range(depth):
             sends[1, j].start()
-
-    @pl.when(opening)
-    def _():
-        flag_copy.start()
 
     forward(0, 1)
     squares(i - 1, range(i - span, i + 2))

time: 29.7 us -> 28.5 us (0.960)
  Pallas kernels: 28.7 us -> 27.5 us
    pallas_call x1, Pallas kernels: 28.7 us -> 27.5 us  [per_device(): pl.pallas_call(functools.partial(purify, (layers, grids, rows, reach, blo...]
where the time goes in v3:
time: 28.5 us; the launch traced here: 28.4 us
  Pallas kernels  27.5 us (96%)
  local copies, waits for them, and re-layouts  0.87 us (3%)
    pallas_call x1, Pallas kernels, per_device(): pl.pallas_call(functools.partial(purify, (layers, grids, rows, reach, blo...  27.5 us
    unnamed x1, local copies, waits for them, and re-layouts  0.87 us

profile of v3, /device:TPU:0, one launch (start us, length us, event | category | flops | bytes accessed | tf_op | source)
XLA Modules:
  0.0 28.4 jit_solution(14631755153003649061)
XLA Ops:
  0.0 27.5 %purify.1 = bf16[10,9,32,128]{3,2,1,0:T(8,128)(2,1)S(1)} custom-call(bf16[10,9,128,128]{3,2,1,0:T(8,128)(2,1)} %x_hbm.1, s32[10,9]{1,0:T(8,128)} %r_hbm.1), custom_call_target="tpu_custom_call" | custom-call | tf_op jit(solution)/shard_map/purify/pallas_call | solution.py:447
  27.5 0.9 %copy.4 = bf16[10,9,32,128]{3,2,1,0:T(8,128)(2,1)} copy(bf16[10,9,32,128]{3,2,1,0:T(8,128)(2,1)S(1)} %purify.1) | data formatting | bytes 1474560
